TPU v7x, 512 devices: a whole 4x8x8 slice. The times are simulated.
512 devices in a mesh: gx: 8 (over z), gy: 8 (over y_lo, core), gz: 8 (over y_hi, x).
Axes of the slice: x: 4, y: 8 (y_hi: 2, y_lo: 4; y = y_hi * 4 + y_lo), z: 8, core: 2. Of those that a mesh axis runs over, the one named last changes fastest.
Arguments:
- x_in: bfloat16 [3072, 5120], P(('gy', 'gx'), 'gz'), may hold values from -190 to 190
- gain: float32 [5120], P('gz'), may hold values from 0.25 to 1.75
- w_up: bfloat16 [5120, 7168], P(('gz', 'gy'), 'gx'), may hold values from -0.078125 to 0.078125
- w_down: bfloat16 [7168, 5120], P(('gx', 'gy'), 'gz'), may hold values from -0.0625 to 0.0625
- d_out: bfloat16 [3072, 5120], P(('gy', 'gx'), 'gz'), may hold values from -1.1953125 to 1.1953125
Outputs:
- d_x: bfloat16 [3072, 5120], P(('gy', 'gx'), 'gz')
- d_w_up: bfloat16 [5120, 7168], P(('gz', 'gy'), 'gx')
- d_w_down: bfloat16 [7168, 5120], P(('gx', 'gy'), 'gz')
- d_gain: float32 [5120], P('gz')
All inputs are finite; a program needn't handle non-finite values.
Results may differ from a plain program's by a relative error of at most 0.02.
Values may be sent and summed in bfloat16 or wider, within the bound.
No kernel may reach another device: no remote copies, remote signals or barrier semaphores. Data moves between devices by JAX's collectives and lax.ppermute only.
A program may use at most 64 MiB of HBM per device.

v0:
```python
import jax
import jax.numpy as jnp
from jax import lax
from jax.sharding import PartitionSpec as P


def gelu_pair(hidden):
    cdf = 0.5 * (1.0 + jax.scipy.special.erf(hidden * 0.7071067811865476))
    slope = cdf + hidden * jnp.exp(-0.5 * hidden * hidden) * 0.3989422804014327
    return (hidden * cdf, slope)


def body(x_in, gain, w_up, w_down, d_out):
    width = x_in.shape[1] * lax.axis_size("gz")
    xf = x_in.astype(jnp.float32)
    total = lax.psum(jnp.sum(xf, axis=1), "gz")
    mean = total / width
    centered = xf - mean[:, None]
    var = lax.psum(jnp.sum(centered * centered, axis=1), "gz") / width
    inv = lax.rsqrt(var + 1e-05)[:, None]
    normed = centered * inv
    z_local = (normed * gain).astype(jnp.bfloat16)
    up_full = lax.all_gather(w_up, "gy", axis=0, tiled=True)
    z_rows = lax.all_gather(z_local, "gx", axis=0, tiled=True)
    part_rows = z_rows
    hidden = lax.psum_scatter(
        jnp.dot(part_rows, up_full, preferred_element_type=jnp.float32).astype(jnp.bfloat16),
        "gz",
        scatter_dimension=0,
        tiled=True,
    ).astype(jnp.float32)
    act_f, slope = gelu_pair(hidden)
    act = act_f.astype(jnp.bfloat16)
    down_full = lax.all_gather(w_down, "gy", axis=0, tiled=True)
    out_rows = lax.all_gather(d_out, "gx", axis=0, tiled=True)
    act_rows = lax.all_gather(act, "gz", axis=0, tiled=True)
    part_rows = out_rows
    d_act = lax.psum_scatter(
        lax.dot_general(
            part_rows, down_full, (((1,), (1,)), ((), ())), preferred_element_type=jnp.float32
        ).astype(jnp.bfloat16),
        "gz",
        scatter_dimension=0,
        tiled=True,
    ).astype(jnp.float32)
    d_hidden = (d_act * slope).astype(jnp.bfloat16)
    hgrad_rows = lax.all_gather(d_hidden, "gz", axis=0, tiled=True)
    columns = act_rows
    d_w_down = lax.psum_scatter(
        lax.dot_general(
            columns, out_rows, (((0,), (0,)), ((), ())), preferred_element_type=jnp.float32
        ).astype(jnp.bfloat16),
        "gy",
        scatter_dimension=0,
        tiled=True,
    )
    columns = z_rows
    d_w_up = lax.psum_scatter(
        lax.dot_general(
            columns, hgrad_rows, (((0,), (0,)), ((), ())), preferred_element_type=jnp.float32
        ).astype(jnp.bfloat16),
        "gy",
        scatter_dimension=0,
        tiled=True,
    )
    part_rows = hgrad_rows
    d_z = lax.psum_scatter(
        lax.dot_general(
            part_rows, up_full, (((1,), (1,)), ((), ())), preferred_element_type=jnp.float32
        ).astype(jnp.bfloat16),
        "gx",
        scatter_dimension=0,
        tiled=True,
    ).astype(jnp.float32)
    d_gain = lax.psum(jnp.sum(d_z * normed, axis=0), ("gx", "gy"))
    d_scaled = d_z * gain
    scaled_sum, cross_sum = lax.psum(
        (jnp.sum(d_scaled, axis=1), jnp.sum(d_scaled * normed, axis=1)), "gz"
    )
    d_x = inv * (d_scaled - scaled_sum[:, None] / width - normed * (cross_sum[:, None] / width))
    return (d_x.astype(jnp.bfloat16), d_w_up, d_w_down, d_gain)


def solution(mesh):
    placed = (
        P(("gy", "gx"), "gz"),
        P("gz"),
        P(("gz", "gy"), "gx"),
        P(("gx", "gy"), "gz"),
        P(("gy", "gx"), "gz"),
    )
    return jax.shard_map(
        body,
        mesh=mesh,
        in_specs=placed,
        out_specs=(P(("gy", "gx"), "gz"), P(("gz", "gy"), "gx"), P(("gx", "gy"), "gz"), P("gz")),
        check_vma=False,
    )
```

profile of v0, /device:TPU:1, one launch (start us, length us, event | category | flops | bytes accessed | tf_op | source)
XLA Modules:
  0.0 543.6 jit_solution(16610349977316155122)
XLA Ops:
  7.2 0.0 all-gather.3.cloned.1.call-start
  7.2 0.7 all-gather.3.cloned.1.call-update
  7.9 0.0 all-gather.5.cloned.1.call-start
  7.9 0.7 all-gather.5.cloned.1.call-update
  8.6 0.0 reduce-scatter.6.cloned.1.call-start
  8.7 27.0 %all_gather.18 = bf16[384,640]{1,0:T(8,128)(2,1)S(1)} all-gather(bf16[48,640]{1,0:T(8,128)(2,1)} %param.9), channel_id=1, replica_groups=mesh['gx'=8,'gy'=8,'gz'=8] {'gx'}, dimensions={0}, use_global_device_ids=true | all-gather | bytes 552960 | tf_op jit(solution)/shard_map/all_gather | solution.py:35
  35.7 0.0 copy-start
  35.7 0.0 copy-start.1
  35.7 17.8 %all-gather.3.cloned.1.call-done = bf16[896,640]{1,0:T(8,128)(2,1)} async-done(((bf16[112,640]{1,0:T(8,128)(2,1)}), bf16[896,640]{1,0:T(8,128)(2,1)}) %all-gather.3.cloned.1.call-update) | async-done | bytes 1146896 | tf_op jit(solution)/shard_map/all_gather | solution.py:34
  53.5 2.9 convolution_convert_fusion.3
  56.4 0.0 reduce-scatter.6.cloned.1.call-update
  56.4 0.0 reduce-scatter.8.cloned.1.call-start
  56.5 0.0 copy-done
  56.5 0.1 convert_reduce_fusion
  56.6 26.6 %psum.35 = f32[48]{0:T(128)S(1)} all-reduce(f32[48]{0:T(128)S(1)} %convert_reduce_fusion), channel_id=1, replica_groups=mesh['gx'=8,'gy'=8,'gz'=8] {'gz'}, use_global_device_ids=true, to_apply=%region_1.0 | all-reduce | flops 48 | bytes 384 | tf_op jit(solution)/shard_map/psum | solution.py:16
  83.2 0.2 fusion.20
  83.4 20.3 %psum.36 = f32[48]{0:T(128)S(1)} all-reduce(f32[48]{0:T(128)S(1)} %fusion.20), channel_id=1, replica_groups=mesh['gx'=8,'gy'=8,'gz'=8] {'gz'}, use_global_device_ids=true, to_apply=%region_3.0 | all-reduce | flops 48 | bytes 384 | tf_op jit(solution)/shard_map/psum | solution.py:19
  103.7 0.0 copy-done.1
  103.7 0.1 fusion.16
  103.8 22.4 %all_gather.20 = bf16[384,640]{1,0:T(8,128)(2,1)S(1)} all-gather(bf16[48,640]{1,0:T(8,128)(2,1)S(1)} %fusion.16), channel_id=1, replica_groups=mesh['gx'=8,'gy'=8,'gz'=8] {'gx'}, dimensions={0}, use_global_device_ids=true | all-gather | bytes 552960 | tf_op jit(solution)/shard_map/all_gather | solution.py:24
  126.3 0.0 all-gather.5.cloned.1.call-done
  126.3 2.9 convolution_convert_fusion.2
  129.2 0.0 copy-start.2
  129.2 0.0 reduce-scatter.8.cloned.1.call-update
  129.2 0.0 reduce-scatter.10.cloned.1.call-start
  129.3 56.7 %reduce-scatter.6.cloned.1.call-done = bf16[48,896]{1,0:T(8,128)(2,1)} async-done(((bf16[384,896]{1,0:T(8,128)(2,1)}), bf16[48,896]{1,0:T(8,128)(2,1)}) %reduce-scatter.6.cloned.1.call-update) | async-done | bytes 86032 | tf_op jit(solution)/shard_map/reduce_scatter | solution.py:38
  185.9 88.3 %reduce-scatter.8.cloned.1.call-done = bf16[48,896]{1,0:T(8,128)(2,1)} async-done(((bf16[384,896]{1,0:T(8,128)(2,1)}), bf16[48,896]{1,0:T(8,128)(2,1)}) %reduce-scatter.8.cloned.1.call-update) | async-done | bytes 86032 | tf_op jit(solution)/shard_map/reduce_scatter | solution.py:26
  274.3 1.0 fusion.8
  275.3 39.4 %all_gather.22 = bf16[384,896]{1,0:T(8,128)(2,1)S(1)} all-gather(bf16[48,896]{1,0:T(8,128)(2,1)S(1)} %get-tuple-element.10), channel_id=1, replica_groups=mesh['gx'=8,'gy'=8,'gz'=8] {'gz'}, dimensions={0}, use_global_device_ids=true | all-gather | bytes 774144 | tf_op jit(solution)/shard_map/all_gather | solution.py:47
  314.7 0.0 copy-done.2
  314.7 1.6 convolution_convert_fusion.4
  316.3 0.0 reduce-scatter.10.cloned.1.call-update
  316.3 0.0 reduce-scatter.14.cloned.1.call-start
  316.4 41.4 %all_gather.23 = bf16[384,896]{1,0:T(8,128)(2,1)S(1)} all-gather(bf16[48,896]{1,0:T(8,128)(2,1)S(1)} %get-tuple-element.9), channel_id=1, replica_groups=mesh['gx'=8,'gy'=8,'gz'=8] {'gz'}, dimensions={0}, use_global_device_ids=true | all-gather | bytes 774144 | tf_op jit(solution)/shard_map/all_gather | solution.py:36
  357.8 1.9 convolution_convert_fusion
  359.7 0.0 reduce-scatter.14.cloned.1.call-update
  359.7 0.0 reduce-scatter.12.cloned.1.call-start
  359.8 1.9 convolution_convert_fusion.1
  361.6 0.0 reduce-scatter.12.cloned.1.call-update
  361.6 0.0 reduce-scatter.10.cloned.1.call-done
  361.7 1.0 fusion.22
  362.7 23.1 %all-reduce = (f32[48]{0:T(128)S(1)}, f32[48]{0:T(128)S(1)}) all-reduce(f32[48]{0:T(128)S(1)} %get-tuple-element.5, f32[48]{0:T(128)S(1)} %get-tuple-element.6), channel_id=1, replica_groups=mesh['gx'=8,'gy'=8,'gz'=8] {'gz'}, use_global_device_ids=true, to_apply=%region_10.0 | all-reduce | flops 96 | bytes 768 | tf_op jit(solution)/shard_map/psum | solution.py:77
  385.9 149.4 %psum.39 = f32[640]{0:T(1024)} all-reduce(f32[640]{0:T(1024)S(1)} %get-tuple-element.4), channel_id=1, replica_groups=mesh['gx'=8,'gy'=8,'gz'=8] {'gx','gy'}, use_global_device_ids=true, to_apply=%region_14.0 | all-reduce | flops 640 | bytes 5120 | tf_op jit(solution)/shard_map/psum | solution.py:75
  535.2 1.6 fusion.19
  536.8 0.0 reduce-scatter.14.cloned.1.call-done
  536.8 0.0 reduce-scatter.12.cloned.1.call-done
  (3 shorter events, 0.0 us)
Async XLA Ops:
  7.2 46.4 %all-gather.3.cloned.1.call-start = ((), (), s32[]{:S(2)}) async-start(), calls=%async_computation.5 | async-start | bytes 1290240 | tf_op jit(solution)/shard_map/all_gather | solution.py:34
  7.9 118.4 %all-gather.5.cloned.1.call-start = ((), (), s32[]{:S(2)}) async-start(), calls=%async_computation.7 | async-start | bytes 1290240 | tf_op jit(solution)/shard_map/all_gather | solution.py:23
  8.6 177.3 %reduce-scatter.6.cloned.1.call-start = ((), (), s32[]{:S(2)}) async-start(), calls=%async_computation.6 | async-start | bytes 774144 | tf_op jit(solution)/shard_map/reduce_scatter | solution.py:38
  35.7 20.8 %copy-start = (bf16[48,640]{1,0:T(8,128)(2,1)S(1)}, bf16[48,640]{1,0:T(8,128)(2,1)}, u32[]{:S(2)}) copy-start(bf16[48,640]{1,0:T(8,128)(2,1)} %param.5) | copy-start | bytes 184324
  35.7 68.0 %copy-start.1 = (f32[640]{0:T(1024)S(1)}, f32[640]{0:T(1024)}, u32[]{:S(2)}) copy-start(f32[640]{0:T(1024)} %param.6) | copy-start | bytes 7684
  56.4 217.8 %reduce-scatter.8.cloned.1.call-start = ((), (), s32[]{:S(2)}) async-start(), calls=%async_computation.8 | async-start | bytes 774144 | tf_op jit(solution)/shard_map/reduce_scatter | solution.py:26
  129.2 185.5 %copy-start.2 = (bf16[640,896]{1,0:T(8,128)(2,1)S(1)}, bf16[640,896]{1,0:T(8,128)(2,1)}, u32[]{:S(2)}) copy-start(bf16[640,896]{1,0:T(8,128)(2,1)} %all-gather.5.cloned.1.call-done) | copy-start | bytes 3440644
  129.2 232.5 %reduce-scatter.10.cloned.1.call-start = ((), (), s32[]{:S(2)}) async-start(), calls=%async_computation.9 | async-start | bytes 552960 | tf_op jit(solution)/shard_map/reduce_scatter | solution.py:67
  316.3 220.5 %reduce-scatter.14.cloned.1.call-start = ((), (), s32[]{:S(2)}) async-start(), calls=%async_computation.11 | async-start | bytes 1290240 | tf_op jit(solution)/shard_map/reduce_scatter | solution.py:49
  359.7 177.1 %reduce-scatter.12.cloned.1.call-start = ((), (), s32[]{:S(2)}) async-start(), calls=%async_computation.10 | async-start | bytes 1290240 | tf_op jit(solution)/shard_map/reduce_scatter | solution.py:58
Sparse Core Ops, SparseCore 0:
  10.1 43.4 all-gather.2
  55.6 39.0 all-gather.4
  99.2 86.6 reduce-scatter.5
  191.0 83.2 reduce-scatter.7
  316.5 40.0 reduce-scatter.9
  360.0 47.1 reduce-scatter.13
  410.9 39.1 reduce-scatter.11
where the time goes:
time: 544 us
  blocking collectives  350 us (64%)
  waiting for transfers between devices  164 us (30%)
  between operations  14.2 us (3%)
  matrix products  11.1 us (2%)
    psum x1, blocking collectives, body(): d_gain = lax.psum(jnp.sum(d_z * normed, axis=0), ('gx', 'gy'))  149 us
    reduce_scatter x1, waiting for transfers between devices, body(): lax.psum_scatter(jnp.dot(part_rows, up_full, preferred_element_type=jnp.f...  88.3 us
    reduce_scatter x1, waiting for transfers between devices, body(): lax.psum_scatter(lax.dot_general(part_rows, down_full, (((1,), (1,)), (()...  56.7 us
    all_gather x1, blocking collectives, body(): act_rows = lax.all_gather(act, 'gz', axis=0, tiled=True)  41.4 us
    all_gather x1, blocking collectives, body(): hgrad_rows = lax.all_gather(d_hidden, 'gz', axis=0, tiled=True)  39.4 us
    all_gather x1, blocking collectives, body(): out_rows = lax.all_gather(d_out, 'gx', axis=0, tiled=True)  27 us
    psum x1, blocking collectives, body(): total = lax.psum(jnp.sum(xf, axis=1), 'gz')  26.6 us
    psum x1, blocking collectives, body(): lax.psum((jnp.sum(d_scaled, axis=1), jnp.sum(d_scaled * normed, axis=1)),...  23.1 us
  transfers between devices with their start and end apart: 7, of which 3 were waited for; matrix products, arithmetic and copies ran while one was open for 2% of the time, Pallas kernels for 0%

commit v1 on v0

--- a/solution.py
+++ b/solution.py
@@ -33,7 +33,6 @@
     act = act_f.astype(jnp.bfloat16)
     down_full = lax.all_gather(w_down, "gy", axis=0, tiled=True)
     out_rows = lax.all_gather(d_out, "gx", axis=0, tiled=True)
-    act_rows = lax.all_gather(act, "gz", axis=0, tiled=True)
     part_rows = out_rows
     d_act = lax.psum_scatter(
         lax.dot_general(
@@ -44,7 +43,11 @@
         tiled=True,
     ).astype(jnp.float32)
     d_hidden = (d_act * slope).astype(jnp.bfloat16)
-    hgrad_rows = lax.all_gather(d_hidden, "gz", axis=0, tiled=True)
+    act_rows, hgrad_rows = jnp.split(
+        lax.all_gather(jnp.concatenate([act, d_hidden], axis=1), "gz", axis=0, tiled=True),
+        [act.shape[1]],
+        axis=1,
+    )
     columns = act_rows
     d_w_down = lax.psum_scatter(
         lax.dot_general(

time: 544 us -> 562 us (1.033)
  waiting for transfers between devices: 164 us -> 262 us
  blocking collectives: 350 us -> 266 us
    all_gather x2 -> x0, blocking collectives: 80.8 us -> none  [the longest x1 41.4 us: body(): act_rows = lax.all_gather(act, 'gz', axis=0, tiled=True)]
    all_gather x0 -> x1, waiting for transfers between devices: none -> 67.5 us  [body(): lax.all_gather(jnp.concatenate([act, d_hidden], axis=1), 'gz', axis=0, ti...]
    reduce_scatter x1, waiting for transfers between devices: 56.7 us -> 88.4 us  [body(): lax.psum_scatter(lax.dot_general(part_rows, down_full, (((1,), (1,)), (()...]
    reduce_scatter x1, waiting for transfers between devices: 0.02 us -> 31.2 us  [body(): lax.psum_scatter(lax.dot_general(part_rows, up_full, (((1,), (1,)), ((),...]
    all_gather x1, waiting for transfers between devices: 17.8 us -> 0.01 us  [body(): down_full = lax.all_gather(w_down, 'gy', axis=0, tiled=True)]
    reduce_scatter x1, waiting for transfers between devices: 88.3 us -> 73.1 us  [body(): lax.psum_scatter(jnp.dot(part_rows, up_full, preferred_element_type=jnp.f...]
    all_gather x1, blocking collectives: 27 us -> 19.4 us  [body(): out_rows = lax.all_gather(d_out, 'gx', axis=0, tiled=True)]
    psum x1, blocking collectives: 149 us -> 143 us  [body(): d_gain = lax.psum(jnp.sum(d_z * normed, axis=0), ('gx', 'gy'))]
  transfers between devices with their start and end apart: 7 -> 8, of which waited for: 3 -> 4; matrix products, arithmetic and copies ran while one was open for 2% -> 3% of each run, Pallas kernels for 0% -> 0%
where the time goes in v1:
time: 562 us; the launch traced here: 561 us
  blocking collectives  266 us (47%)
  waiting for transfers between devices  262 us (47%)
  between operations  14.2 us (3%)
  matrix products  12.3 us (2%)
  other arithmetic  7.2 us (1%)
    psum x1, blocking collectives, body(): d_gain = lax.psum(jnp.sum(d_z * normed, axis=0), ('gx', 'gy'))  143 us
    reduce_scatter x1, waiting for transfers between devices, body(): lax.psum_scatter(lax.dot_general(part_rows, down_full, (((1,), (1,)), (()...  88.4 us
    reduce_scatter x1, waiting for transfers between devices, body(): lax.psum_scatter(jnp.dot(part_rows, up_full, preferred_element_type=jnp.f...  73.1 us
    all_gather x1, waiting for transfers between devices, body(): lax.all_gather(jnp.concatenate([act, d_hidden], axis=1), 'gz', axis=0, ti...  67.5 us
    reduce_scatter x1, waiting for transfers between devices, body(): lax.psum_scatter(lax.dot_general(part_rows, up_full, (((1,), (1,)), ((),...  31.2 us
    psum x1, blocking collectives, body(): total = lax.psum(jnp.sum(xf, axis=1), 'gz')  29 us
    psum x1, blocking collectives, body(): lax.psum((jnp.sum(d_scaled, axis=1), jnp.sum(d_scaled * normed, axis=1)),...  27.7 us
    all_gather x1, blocking collectives, body(): z_rows = lax.all_gather(z_local, 'gx', axis=0, tiled=True)  26.6 us
  transfers between devices with their start and end apart: 8, of which 4 were waited for; matrix products, arithmetic and copies ran while one was open for 3% of the time, Pallas kernels for 0%

profile of v1, /device:TPU:1, one launch (start us, length us, event | category | flops | bytes accessed | tf_op | source)
XLA Modules:
  0.0 561.5 jit_solution(7194614212154251674)
XLA Ops:
  7.2 0.0 all-gather.4.cloned.1.call-start
  7.2 0.7 all-gather.4.cloned.1.call-update
  7.9 0.0 all-gather.6.cloned.1.call-start
  7.9 0.7 all-gather.6.cloned.1.call-update
  8.6 0.0 reduce-scatter.6.cloned.1.call-start
  8.7 0.9 convert_reduce_fusion
  9.6 29.0 %psum.35 = f32[48]{0:T(128)S(1)} all-reduce(f32[48]{0:T(128)S(1)} %convert_reduce_fusion), channel_id=1, replica_groups=mesh['gx'=8,'gy'=8,'gz'=8] {'gz'}, use_global_device_ids=true, to_apply=%region_1.0 | all-reduce | flops 48 | bytes 384 | tf_op jit(solution)/shard_map/psum | solution.py:16
  38.6 1.0 fusion.23
  39.6 20.3 %psum.36 = f32[48]{0:T(128)S(1)} all-reduce(f32[48]{0:T(128)S(1)} %fusion.23), channel_id=1, replica_groups=mesh['gx'=8,'gy'=8,'gz'=8] {'gz'}, use_global_device_ids=true, to_apply=%region_3.0 | all-reduce | flops 48 | bytes 384 | tf_op jit(solution)/shard_map/psum | solution.py:19
  59.9 0.9 fusion.19
  60.9 26.6 %all_gather.15 = bf16[384,640]{1,0:T(8,128)(2,1)S(1)} all-gather(bf16[48,640]{1,0:T(8,128)(2,1)S(1)} %fusion.19), channel_id=1, replica_groups=mesh['gx'=8,'gy'=8,'gz'=8] {'gx'}, dimensions={0}, use_global_device_ids=true | all-gather | bytes 552960 | tf_op jit(solution)/shard_map/all_gather | solution.py:24
  87.5 0.0 copy-start.1
  87.5 0.0 all-gather.4.cloned.1.call-done
  87.5 2.9 convolution_convert_fusion.3
  90.4 0.0 reduce-scatter.6.cloned.1.call-update
  90.4 0.0 reduce-scatter.8.cloned.1.call-start
  90.5 0.0 copy-done.1
  90.5 19.4 %all_gather.17 = bf16[384,640]{1,0:T(8,128)(2,1)S(1)} all-gather(bf16[48,640]{1,0:T(8,128)(2,1)S(1)} %copy-done.1), channel_id=1, replica_groups=mesh['gx'=8,'gy'=8,'gz'=8] {'gx'}, dimensions={0}, use_global_device_ids=true | all-gather | bytes 552960 | tf_op jit(solution)/shard_map/all_gather | solution.py:35
  109.8 0.0 all-gather.6.cloned.1.call-done
  109.8 2.9 convolution_convert_fusion.2
  112.7 0.0 copy-start.4
  112.7 0.0 reduce-scatter.8.cloned.1.call-update
  112.8 0.0 all-gather.8.cloned.1.call-start
  112.8 73.1 %reduce-scatter.6.cloned.1.call-done = bf16[48,896]{1,0:T(8,128)(2,1)} async-done(((bf16[384,896]{1,0:T(8,128)(2,1)}), bf16[48,896]{1,0:T(8,128)(2,1)}) %reduce-scatter.6.cloned.1.call-update) | async-done | bytes 86032 | tf_op jit(solution)/shard_map/reduce_scatter | solution.py:26
  186.0 88.4 %reduce-scatter.8.cloned.1.call-done = bf16[48,896]{1,0:T(8,128)(2,1)} async-done(((bf16[384,896]{1,0:T(8,128)(2,1)}), bf16[48,896]{1,0:T(8,128)(2,1)}) %reduce-scatter.8.cloned.1.call-update) | async-done | bytes 86032 | tf_op jit(solution)/shard_map/reduce_scatter | solution.py:37
  274.4 1.0 fusion.6
  275.4 0.7 pad_maximum_fusion
  276.1 0.0 all-gather.8.cloned.1.call-update
  276.1 0.0 reduce-scatter.10.cloned.1.call-start
  276.1 67.5 %all-gather.8.cloned.1.call-done = bf16[384,1792]{1,0:T(8,128)(2,1)} async-done(((bf16[48,1792]{1,0:T(8,128)(2,1)}), bf16[384,1792]{1,0:T(8,128)(2,1)}) %all-gather.8.cloned.1.call-update) | async-done | bytes 1376272 | tf_op jit(solution)/shard_map/all_gather | solution.py:47
  343.7 0.0 copy-done.4
  343.7 0.0 copy-start.3
  343.7 2.8 convolution_convert_fusion.4
  346.5 0.0 reduce-scatter.10.cloned.1.call-update
  346.5 0.0 reduce-scatter.12.cloned.1.call-start
  346.6 0.0 copy-done.3
  346.6 1.9 convolution_convert_fusion.1
  348.4 0.0 reduce-scatter.12.cloned.1.call-update
  348.5 0.0 reduce-scatter.14.cloned.1.call-start
  348.5 1.9 convolution_convert_fusion
  350.4 0.0 reduce-scatter.14.cloned.1.call-update
  350.4 31.2 %reduce-scatter.10.cloned.1.call-done = bf16[48,640]{1,0:T(8,128)(2,1)} async-done(((bf16[384,640]{1,0:T(8,128)(2,1)}), bf16[48,640]{1,0:T(8,128)(2,1)}) %reduce-scatter.10.cloned.1.call-update) | async-done | bytes 61456 | tf_op jit(solution)/shard_map/reduce_scatter | solution.py:70
  381.6 0.0 copy-done
  381.6 0.0 copy-done.2
  381.6 1.0 fusion.25
  382.6 27.7 %all-reduce = (f32[48]{0:T(128)S(1)}, f32[48]{0:T(128)S(1)}) all-reduce(f32[48]{0:T(128)S(1)} %get-tuple-element.5, f32[48]{0:T(128)S(1)} %get-tuple-element.6), channel_id=1, replica_groups=mesh['gx'=8,'gy'=8,'gz'=8] {'gz'}, use_global_device_ids=true, to_apply=%region_10.0 | all-reduce | flops 96 | bytes 768 | tf_op jit(solution)/shard_map/psum | solution.py:80
  410.3 142.7 %psum.39 = f32[640]{0:T(1024)} all-reduce(f32[640]{0:T(1024)S(1)} %get-tuple-element.4), channel_id=1, replica_groups=mesh['gx'=8,'gy'=8,'gz'=8] {'gx','gy'}, use_global_device_ids=true, to_apply=%region_14.0 | all-reduce | flops 640 | bytes 5120 | tf_op jit(solution)/shard_map/psum | solution.py:78
  553.1 1.6 fusion.22
  (7 shorter events, 0.0 us)
Async XLA Ops:
  7.2 80.3 %all-gather.4.cloned.1.call-start = ((), (), s32[]{:S(2)}) async-start(), calls=%async_computation.5 | async-start | bytes 1290240 | tf_op jit(solution)/shard_map/all_gather | solution.py:23
  7.9 101.9 %all-gather.6.cloned.1.call-start = ((), (), s32[]{:S(2)}) async-start(), calls=%async_computation.7 | async-start | bytes 1290240 | tf_op jit(solution)/shard_map/all_gather | solution.py:34
  8.6 177.3 %reduce-scatter.6.cloned.1.call-start = ((), (), s32[]{:S(2)}) async-start(), calls=%async_computation.6 | async-start | bytes 774144 | tf_op jit(solution)/shard_map/reduce_scatter | solution.py:26
  87.5 3.0 copy-start.1
  90.4 183.9 %reduce-scatter.8.cloned.1.call-start = ((), (), s32[]{:S(2)}) async-start(), calls=%async_computation.8 | async-start | bytes 774144 | tf_op jit(solution)/shard_map/reduce_scatter | solution.py:37
  112.7 231.0 %copy-start.4 = (bf16[640,896]{1,0:T(8,128)(2,1)S(1)}, bf16[640,896]{1,0:T(8,128)(2,1)}, u32[]{:S(2)}) copy-start(bf16[640,896]{1,0:T(8,128)(2,1)} %all-gather.4.cloned.1.call-done) | copy-start | bytes 3440644
  112.8 230.9 %all-gather.8.cloned.1.call-start = ((), (), s32[]{:S(2)}) async-start(), calls=%async_computation.9 | async-start | bytes 1548288 | tf_op jit(solution)/shard_map/all_gather | solution.py:47
  276.1 105.5 %reduce-scatter.10.cloned.1.call-start = ((), (), s32[]{:S(2)}) async-start(), calls=%async_computation.10 | async-start | bytes 552960 | tf_op jit(solution)/shard_map/reduce_scatter | solution.py:70
  343.7 2.9 copy-start.3
  346.5 208.1 %reduce-scatter.12.cloned.1.call-start = ((), (), s32[]{:S(2)}) async-start(), calls=%async_computation.11 | async-start | bytes 1290240 | tf_op jit(solution)/shard_map/reduce_scatter | solution.py:61
  348.5 206.2 %reduce-scatter.14.cloned.1.call-start = ((), (), s32[]{:S(2)}) async-start(), calls=%async_computation.12 | async-start | bytes 1290240 | tf_op jit(solution)/shard_map/reduce_scatter | solution.py:52
  350.4 31.2 %copy-start = (bf16[48,640]{1,0:T(8,128)(2,1)S(1)}, bf16[48,640]{1,0:T(8,128)(2,1)}, u32[]{:S(2)}) copy-start(bf16[48,640]{1,0:T(8,128)(2,1)} %param.5) | copy-start | bytes 184324
  350.4 31.2 %copy-start.2 = (f32[640]{0:T(1024)S(1)}, f32[640]{0:T(1024)}, u32[]{:S(2)}) copy-start(f32[640]{0:T(1024)} %param.6) | copy-start | bytes 7684
Sparse Core Ops, SparseCore 0:
  10.1 43.7 all-gather.3
  56.0 38.5 all-gather.5
  99.1 86.8 reduce-scatter.5
  191.0 83.3 reduce-scatter.7
  277.4 66.2 all-gather.7
  346.6 34.8 reduce-scatter.9
  385.2 41.1 reduce-scatter.11
  430.0 39.8 reduce-scatter.13
